TPU v7x, 32 devices: a whole 2x2x4 slice. The times are simulated.
32 devices in a mesh: row: 2 (over y), col: 16 (over z, x, core).
Axes of the slice: x: 2, y: 2, z: 4, core: 2. Of those that a mesh axis runs over, the one named last changes fastest.
Arguments:
- object_field: float32 [2, 512, 4096], P(None, 'row', 'col'), may hold values from -6 to 6
- probe_field: float32 [2, 256, 256], replicated, may hold values from -4.2 to 4.2
- amplitudes: bfloat16 [2, 16, 6, 256, 256], P('row', 'col'), may hold values from 0 to 2
- offsets: int32 [2, 16, 6, 2], P('row', 'col'), may hold values from 0 to 256
- counts: int32 [2, 16], P('row', 'col'), may hold values from 2 to 6
Outputs:
- updated_object: float32 [2, 512, 4096], P(None, 'row', 'col')
Inputs may be any that keep to these rules, and one draw needn't show every extreme that they name: Tile (r, c) uses slots 0 to counts[r, c] - 1; offsets and amplitudes of the other slots are ignored.
All inputs are finite; a program needn't handle non-finite values.
Results may differ from a plain program's by a relative error of at most 0.0021.
Values sent between devices are 32-bit elements; how exact they have to be, the bound alone decides.
A program may use at most 64 MiB of HBM per device.

v0:
```python
import functools
import math

import jax
import jax.numpy as jnp
import numpy as np
from jax import lax
from jax.experimental import pallas as pl
from jax.experimental.pallas import tpu as pltpu
from jax.sharding import PartitionSpec as P

TILE = 256
RIM = 128
MAXPOS = 6
ITERS = 2
LANES = 128
CHUNK = 32
VMEM_LIMIT = 28 * 1024 * 1024
WIRE_COST = pl.CostEstimate(flops=0, transcendentals=0, bytes_accessed=40_000_000)

smooth_term = 0.25
step_size = 0.5
regular_term = 1.0

AXES = ("row", "col")
SIDES = [(-1, 0), (1, 0), (0, -1), (0, 1), (-1, -1), (-1, 1), (1, -1), (1, 1)]


def dft_tables():
    positions = np.arange(TILE)
    phase_step = (positions[:, None] * positions[None, :]) % TILE
    angle = phase_step.astype(np.float32) * np.float32(2.0 * math.pi / TILE)
    scale = np.float32(1.0 / math.sqrt(TILE))
    real = np.cos(angle).astype(np.float32) * scale
    imag = -np.sin(angle).astype(np.float32) * scale
    return np.stack([real, imag]).astype(jnp.bfloat16)


def edge(step, length):
    if step < 0:
        return slice(0, RIM)
    if step > 0:
        return slice(length - RIM, length)
    return slice(0, length)


def zone(step):
    return (slice(0, RIM), slice(RIM, RIM + TILE), slice(RIM + TILE, 2 * RIM + TILE))[step + 1]


def shape_of(planes, side):
    return (planes, TILE if side[0] == 0 else RIM, TILE if side[1] == 0 else RIM)


def inside(row, col):
    rows, cols = lax.axis_size("row"), lax.axis_size("col")
    return (row >= 0) & (row < rows) & (col >= 0) & (col < cols)


def greet(row, col):
    barrier = pltpu.get_barrier_semaphore()
    peers = 0
    for down, right in SIDES[:4]:
        present = inside(row + down, col + right)
        peers = peers + jnp.where(present, 1, 0)

        @pl.when(present)
        def _():
            pl.semaphore_signal(
                barrier,
                inc=1,
                device_id=(row + down, col + right),
                device_id_type=pl.DeviceIdType.MESH,
            )

    pl.semaphore_wait(barrier, peers)


def transfer(source, landing, sends, receives, slot, device):
    return pltpu.make_async_remote_copy(
        src_ref=source,
        dst_ref=landing,
        send_sem=sends.at[slot],
        recv_sem=receives.at[slot],
        device_id=device,
        device_id_type=pl.DeviceIdType.MESH,
    )


def half_of(right):
    return slice(0, LANES) if right < 0 else slice(LANES, 2 * LANES)


def half_slot(down, right):
    return (0 if down < 0 else 1) + (0 if right < 0 else 8)


CORNERS = SIDES[4:]


def halo_kernel(field, *refs):
    outs = refs[:8]
    sends, receives = refs[8:]
    row, col = lax.axis_index("row"), lax.axis_index("col")
    greet(row, col)

    def row_copy(down, right, device):
        half = half_of(right)
        return transfer(
            field.at[:, edge(down, TILE), half],
            outs[SIDES.index((down, 0))].at[:, :, half],
            sends,
            receives,
            half_slot(down, right),
            device,
        )

    def col_copy(right, device):
        at = SIDES.index((0, right))
        return transfer(
            field.at[:, :, edge(right, TILE)], outs[at], sends, receives, at, device
        )

    def corner_copy(down, right, device):
        at = SIDES.index((down, right))
        landed = outs[SIDES.index((down, 0))].at[:, :, half_of(right)]
        return transfer(landed, outs[at], sends, receives, at, device)

    for down, right in CORNERS:

        @pl.when(inside(row + down, col))
        def _():
            row_copy(down, right, (row + down, col)).start()

    for right in (-1, 1):

        @pl.when(inside(row, col + right))
        def _():
            col_copy(right, (row, col + right)).start()

    for (down, right), out in zip(SIDES, outs):

        @pl.when(jnp.logical_not(inside(row - down, col - right)))
        def _():
            out[...] = jnp.zeros(out.shape, jnp.float32)

    for down, right in CORNERS:

        @pl.when(inside(row - down, col))
        def _():
            row_copy(down, right, (row - down, col)).wait_recv()

        @pl.when(inside(row - down, col) & inside(row, col + right))
        def _():
            corner_copy(down, right, (row, col + right)).start()

    for right in (-1, 1):

        @pl.when(inside(row, col - right))
        def _():
            col_copy(right, (row, col - right)).wait_recv()

    for down, right in CORNERS:

        @pl.when(inside(row - down, col - right))
        def _():
            corner_copy(down, right, (row, col - right)).wait_recv()

    for down, right in CORNERS:

        @pl.when(inside(row + down, col))
        def _():
            row_copy(down, right, (row + down, col)).wait_send()

        @pl.when(inside(row - down, col) & inside(row, col + right))
        def _():
            corner_copy(down, right, (row, col + right)).wait_send()

    for right in (-1, 1):

        @pl.when(inside(row, col + right))
        def _():
            col_copy(right, (row, col + right)).wait_send()


def gradient_kernel(
    planes, offs, cnt, own, *refs
):
    halos = refs[:8]
    probe, amps, table = refs[8:11]
    center_out = refs[11]
    outs = refs[12:20]
    ext, canvas, left_m, right_m, wave, half, full = refs[20:]

    real, imag = table[0], table[1]
    left_m[:TILE, :TILE] = real
    left_m[:TILE, TILE:] = -imag
    left_m[TILE:, :TILE] = imag
    left_m[TILE:, TILE:] = real
    right_m[:TILE, :TILE] = real
    right_m[:TILE, TILE:] = imag
    right_m[TILE:, :TILE] = -imag
    right_m[TILE:, TILE:] = real

    canvas[...] = jnp.zeros_like(canvas)
    ext[:, 4] = jnp.zeros_like(ext[:, 4])
    for block in range(2):
        ext[:, 1 + block, RIM : RIM + TILE, :] = own[:, :, block * LANES : (block + 1) * LANES]
    for (down, right), halo in zip(SIDES, halos):
        rows = zone(-down)
        if right == 0:
            ext[:, 1, rows, :] = halo[:, :, :LANES]
            ext[:, 2, rows, :] = halo[:, :, LANES:]
        else:
            ext[:, 3 if right < 0 else 0, rows, :] = halo[...]

    lane = lax.broadcasted_iota(jnp.int32, (CHUNK, LANES), 1)

    def one_slot(slot, carry):
        top = offs[0, slot]
        left = offs[1, slot]
        first = left // LANES
        shift = left % LANES
        back = (LANES - shift) % LANES
        keep = lane < LANES - shift
        late = lane >= shift
        for at in range(0, TILE, CHUNK):
            rows = pl.ds(top + at, CHUNK)
            parts = []
            for p in range(2):
                rolled = [
                    pltpu.roll(ext[p, first + b, rows, :], back, 1) for b in range(3)
                ]
                parts.append([jnp.where(keep, rolled[b], rolled[b + 1]) for b in range(2)])
            for b in range(2):
                cols = slice(b * LANES, (b + 1) * LANES)
                pr = probe[0, at : at + CHUNK, cols]
                pi = probe[1, at : at + CHUNK, cols]
                wr, wi = parts[0][b], parts[1][b]
                wave[at : at + CHUNK, cols] = (pr * wr - pi * wi).astype(jnp.bfloat16)
                wave[TILE + at : TILE + at + CHUNK, cols] = (pr * wi + pi * wr).astype(jnp.bfloat16)

        def by_rows(matrix):
            product = jnp.dot(matrix[...], wave[...], preferred_element_type=jnp.float32)
            half[:, :TILE] = product[:TILE].astype(jnp.bfloat16)
            half[:, TILE:] = product[TILE:].astype(jnp.bfloat16)

        def by_cols(matrix):
            full[...] = jnp.dot(half[...], matrix[...], preferred_element_type=jnp.float32)

        by_rows(left_m)
        by_cols(right_m)
        for at in range(0, TILE, CHUNK):
            sr = full[at : at + CHUNK, :TILE]
            si = full[at : at + CHUNK, TILE:]
            amp = amps[slot, at : at + CHUNK, :].astype(jnp.float32)
            factor = 1.0 - amp * lax.rsqrt(sr * sr + si * si + smooth_term)
            wave[at : at + CHUNK, :] = (sr * factor).astype(jnp.bfloat16)
            wave[TILE + at : TILE + at + CHUNK, :] = (si * factor).astype(jnp.bfloat16)
        by_rows(right_m)
        by_cols(left_m)
        for at in range(0, TILE, CHUNK):
            rows = pl.ds(top + at, CHUNK)
            pieces = [[] for _ in range(planes)]
            for b in range(2):
                cols = slice(b * LANES, (b + 1) * LANES)
                pr = probe[0, at : at + CHUNK, cols]
                pi = probe[1, at : at + CHUNK, cols]
                br = full[at : at + CHUNK, cols]
                bi = full[at : at + CHUNK, TILE + b * LANES : TILE + (b + 1) * LANES]
                pieces[0].append(pltpu.roll(pr * br + pi * bi, shift, 1))
                pieces[1].append(pltpu.roll(pr * bi - pi * br, shift, 1))
                if planes > 2:
                    pieces[2].append(pltpu.roll(pr * pr + pi * pi, shift, 1))
            for p in range(planes):
                a, b = pieces[p]
                canvas[p, first, rows, :] += jnp.where(late, a, 0.0)
                canvas[p, first + 1, rows, :] += jnp.where(late, b, a)
                canvas[p, first + 2, rows, :] += jnp.where(late, 0.0, b)
        return carry

    lax.fori_loop(0, cnt[0], one_slot, 0)

    center_out[:, :, :LANES] = canvas[:, 1, RIM : RIM + TILE, :]
    center_out[:, :, LANES:] = canvas[:, 2, RIM : RIM + TILE, :]
    for (down, right), out in zip(SIDES, outs):
        rows = zone(down)
        if right == 0:
            out[:, :, :LANES] = canvas[:, 1, rows, :]
            out[:, :, LANES:] = canvas[:, 2, rows, :]
        else:
            out[...] = canvas[:, 0 if right < 0 else 3, rows, :]


def update_kernel(first, own, center, *refs):
    pieces = refs[:8]
    refs = refs[8:]
    if not first:
        scale_in = refs[0]
        refs = refs[1:]
    new = refs[0]
    landed = refs[-13:-5]
    sums = refs[-5:-3]
    total, sends, receives = refs[-3:]
    row, col = lax.axis_index("row"), lax.axis_index("col")
    greet(row, col)

    def corner_copy(down, right, device):
        at = SIDES.index((down, right))
        return transfer(pieces[at], landed[at], sends, receives, at, device)

    def col_copy(right, device):
        at = SIDES.index((0, right))
        return transfer(pieces[at], landed[at], sends, receives, at, device)

    def row_copy(down, right, device):
        at = SIDES.index((down, 0))
        half = half_of(right)
        return transfer(
            sums[at].at[:, :, half],
            landed[at].at[:, :, half],
            sends,
            receives,
            half_slot(down, right),
            device,
        )

    for down, right in CORNERS:

        @pl.when(inside(row + down, col + right))
        def _():
            corner_copy(down, right, (row, col + right)).start()

    for right in (-1, 1):

        @pl.when(inside(row, col + right))
        def _():
            col_copy(right, (row, col + right)).start()

    for at, (down, right) in enumerate(SIDES[:4]):

        @pl.when(jnp.logical_not(inside(row - down, col - right)))
        def _():
            landed[at][...] = jnp.zeros(landed[at].shape, jnp.float32)

    for at in range(2):
        sums[at][...] = pieces[at][...]
    def send_half(side):
        half = half_of(side)
        for down in (-1, 1):

            @pl.when(inside(row + down, col) & inside(row, col + side))
            def _():
                corner_copy(down, -side, (row, col + side)).wait_recv()
                landing = landed[SIDES.index((down, -side))]
                sums[SIDES.index((down, 0))][:, :, half] += landing[...]

        total[:, :, half] = center[:, :, half]
        for down in (-1, 1):

            @pl.when(inside(row + down, col))
            def _():
                row_copy(down, side, (row + down, col)).start()

    @pl.when(col % 2 == 1)
    def _():
        send_half(-1)
        send_half(1)

    @pl.when(col % 2 == 0)
    def _():
        send_half(1)
        send_half(-1)

    for right in (-1, 1):

        @pl.when(inside(row, col - right))
        def _():
            col_copy(right, (row, col - right)).wait_recv()

        total[:, :, edge(-right, TILE)] += landed[SIDES.index((0, right))][...]

    for down, right in CORNERS:

        @pl.when(inside(row - down, col))
        def _():
            row_copy(down, right, (row - down, col)).wait_recv()

    for down in (-1, 1):
        total[:, edge(-down, TILE), :] += landed[SIDES.index((down, 0))][...]

    for down, right in CORNERS:

        @pl.when(inside(row + down, col + right))
        def _():
            corner_copy(down, right, (row, col + right)).wait_send()

        @pl.when(inside(row + down, col))
        def _():
            row_copy(down, right, (row + down, col)).wait_send()

    for right in (-1, 1):

        @pl.when(inside(row, col + right))
        def _():
            col_copy(right, (row, col + right)).wait_send()

    if first:
        scale = step_size / (total[2] + regular_term)
        refs[1][...] = scale
    else:
        scale = scale_in[...]
    for p in range(2):
        new[p] = own[p] - total[p] * scale


def vmem(count):
    return [pl.BlockSpec(memory_space=pltpu.VMEM)] * count


def dma_sems():
    return [pltpu.SemaphoreType.DMA((10,))] * 2


def f32(shape):
    return jax.ShapeDtypeStruct(shape, jnp.float32)


def per_device(object_field, probe_field, amplitudes, offsets, counts):
    table = jnp.asarray(dft_tables())
    offs = offsets.reshape(MAXPOS, 2).T
    cnt = counts.reshape(1)
    amps = amplitudes.reshape(MAXPOS, TILE, TILE)
    field = object_field
    edge_shapes = [f32(shape_of(2, side)) for side in SIDES]
    scale = None
    for iteration in range(ITERS):
        first = iteration == 0
        planes = 3 if first else 2
        halos = pl.pallas_call(
            halo_kernel,
            out_shape=edge_shapes,
            in_specs=vmem(1),
            out_specs=vmem(8),
            scratch_shapes=dma_sems(),
            compiler_params=pltpu.CompilerParams(collective_id=0, has_side_effects=True, vmem_limit_bytes=VMEM_LIMIT),
            cost_estimate=WIRE_COST,
            name="halo",
        )(field)
        center, *pieces = pl.pallas_call(
            functools.partial(gradient_kernel, planes),
            out_shape=[f32((planes, TILE, TILE))] + [f32(shape_of(planes, s)) for s in SIDES],
            in_specs=[pl.BlockSpec(memory_space=pltpu.SMEM)] * 2 + vmem(12),
            out_specs=vmem(9),
            scratch_shapes=[
                pltpu.VMEM((2, 5, 2 * TILE, LANES), jnp.float32),
                pltpu.VMEM((planes, 5, 2 * TILE, LANES), jnp.float32),
                pltpu.VMEM((2 * TILE, 2 * TILE), jnp.bfloat16),
                pltpu.VMEM((2 * TILE, 2 * TILE), jnp.bfloat16),
                pltpu.VMEM((2 * TILE, TILE), jnp.bfloat16),
                pltpu.VMEM((TILE, 2 * TILE), jnp.bfloat16),
                pltpu.VMEM((TILE, 2 * TILE), jnp.float32),
            ],
            compiler_params=pltpu.CompilerParams(vmem_limit_bytes=VMEM_LIMIT),
            name=f"gradient{iteration}",
        )(offs, cnt, field, *halos, probe_field, amps, table)
        operands = [field, center, *pieces] + ([] if first else [scale])
        shapes = [f32((2, TILE, TILE))]
        if first:
            shapes.append(f32((TILE, TILE)))
        results = pl.pallas_call(
            functools.partial(update_kernel, first),
            out_shape=shapes,
            in_specs=vmem(len(operands)),
            out_specs=vmem(len(shapes)),
            scratch_shapes=[pltpu.VMEM(shape_of(planes, s), jnp.float32) for s in SIDES]
            + [pltpu.VMEM((planes, RIM, TILE), jnp.float32)] * 2
            + [pltpu.VMEM((planes, TILE, TILE), jnp.float32)]
            + dma_sems(),
            compiler_params=pltpu.CompilerParams(
                collective_id=1 + iteration,
                has_side_effects=True,
                vmem_limit_bytes=VMEM_LIMIT,
            ),
            cost_estimate=WIRE_COST,
            name=f"update{iteration}",
        )(*operands)
        field = results[0]
        if first:
            scale = results[1]
    return field


def solution(mesh):
    in_specs = (
        P(None, "row", "col"),
        P(),
        P("row", "col", None, None, None),
        P("row", "col", None, None),
        P("row", "col"),
    )
    out_specs = P(None, "row", "col")
    return jax.shard_map(
        per_device, mesh=mesh, in_specs=in_specs, out_specs=out_specs, check_vma=False
    )
```

profile of v0, /device:TPU:9, one launch (start us, length us, event | category | flops | bytes accessed | tf_op | source)
XLA Modules:
  0.0 80.5 jit_solution(10652340646204292441)
XLA Ops:
  0.7 0.0 copy-start
  0.7 1.0 %copy-done = f32[2,256,256]{2,1,0:T(8,128)S(1)} copy-done((f32[2,256,256]{2,1,0:T(8,128)S(1)}, f32[2,256,256]{2,1,0:T(8,128)}, u32[]{:S(2)}) %copy-start) | copy-done | bytes 524312
  1.7 0.0 copy-start.3
  1.7 11.9 %halo.2 = (f32[2,128,256]{2,1,0:T(8,128)S(1)}, f32[2,128,256]{2,1,0:T(8,128)S(1)}, f32[2,256,128]{2,1,0:T(8,128)S(1)}, f32[2,256,128]{2,1,0:T(8,128)S(1)}, f32[2...) custom-call(f32[2,256,256]{2,1,0:T(8,128)S(1)} %copy-done), custom_call_target="tpu_custom_call" | custom-call | bytes 40000000 | tf_op jit(solution)/shard_map/halo/pallas_call | solution.py:440
  13.7 0.0 copy-start.6
  13.7 0.0 copy-done.3
  13.7 0.7 copy-done.6
  14.3 0.0 copy-start.1
  14.3 1.1 %copy-done.1 = bf16[1,1,6,256,256]{4,3,2,1,0:T(8,128)(2,1)S(1)} copy-done((bf16[1,1,6,256,256]{4,3,2,1,0:T(8,128)(2,1)S(1)}, bf16[1,1,6,256,256]{4,3,2,1,0:T(8,128)(2,1)}, u32[]{:S(2)}) %copy-start.1) | copy-done | bytes 786456
  15.5 0.0 copy-start.4
  15.5 0.9 %copy-done.4 = bf16[2,256,256]{2,1,0:T(8,128)(2,1)S(1)} copy-done((bf16[2,256,256]{2,1,0:T(8,128)(2,1)S(1)}, bf16[2,256,256]{2,1,0:T(8,128)(2,1)}, u32[]{:S(2)}) %copy-start.4) | copy-done | bytes 262168
  16.4 8.4 %gradient0.1 = (f32[3,256,256]{2,1,0:T(8,128)S(1)}, f32[3,128,256]{2,1,0:T(8,128)S(1)}, f32[3,128,256]{2,1,0:T(8,128)S(1)}, f32[3,256,128]{2,1,0:T(8,128)S(1)}, ...) custom-call(s32[2,6]{1,0:T(2,128)S(1)} %bitcast.9, ...), custom_call_target="tpu_custom_call" | custom-call | tf_op jit(solution)/shard_map/gradient0/pallas_call | solution.py:450
  24.9 0.0 copy-start.2
  24.9 20.0 %update0.1 = (f32[2,256,256]{2,1,0:T(8,128)S(1)}, f32[256,256]{1,0:T(8,128)S(1)}) custom-call(f32[2,256,256]{2,1,0:T(8,128)S(1)} %copy-done, f32[3,256,256]{2,1,0:T(8,128)S(1)} %get-tuple-element.49.center, f32[3,128,256]{2,1,0:T(8,128)S(1)} %get-tuple-element.50.refs_0_, f32[3,128,256]{2,1,0:T(8,128)S(1)} %get-tuple-element.51.refs_1_, ...), custom_call_target="tpu_custom_call" | custom-call | bytes 40000000 | tf_op jit(solution)/shard_map/update0/pallas_call | solution.py:471
  44.9 0.0 copy-start.5
  44.9 11.7 %halo.3 = (f32[2,128,256]{2,1,0:T(8,128)S(1)}, f32[2,128,256]{2,1,0:T(8,128)S(1)}, f32[2,256,128]{2,1,0:T(8,128)S(1)}, f32[2,256,128]{2,1,0:T(8,128)S(1)}, f32[2...) custom-call(f32[2,256,256]{2,1,0:T(8,128)S(1)} %get-tuple-element.58, ...), custom_call_target="tpu_custom_call" | custom-call | bytes 40000000 | tf_op jit(solution)/shard_map/halo/pallas_call | solution.py:440
  56.6 0.0 copy-done.2
  56.6 0.0 copy-done.5
  56.6 8.3 %gradient1.1 = (f32[2,256,256]{2,1,0:T(8,128)S(1)}, f32[2,128,256]{2,1,0:T(8,128)S(1)}, f32[2,128,256]{2,1,0:T(8,128)S(1)}, f32[2,256,128]{2,1,0:T(8,128)S(1)}, ...) custom-call(s32[2,6]{1,0:T(2,128)S(1)} %bitcast.10, ...), custom_call_target="tpu_custom_call" | custom-call | tf_op jit(solution)/shard_map/gradient1/pallas_call | solution.py:450
  64.9 14.8 %update1.1 = f32[2,256,256]{2,1,0:T(8,128)S(1)} custom-call(f32[2,256,256]{2,1,0:T(8,128)S(1)} %get-tuple-element.58.field.own, f32[2,256,256]{2,1,0:T(8,128)S(1)} %get-tuple-element.67.center, f32[2,128,256]{2,1,0:T(8,128)S(1)} %get-tuple-element.68.refs_0_, f32[2,128,256]{2,1,0:T(8,128)S(1)} %get-tuple-element.69.refs_1_, ...), custom_call_target="tpu_custom_call" | custom-call | bytes 40000000 | tf_op jit(solution)/shard_map/update1/pallas_call | solution.py:471
  79.7 0.8 copy.9
Async XLA Ops:
  0.7 1.0 %copy-start = (f32[2,256,256]{2,1,0:T(8,128)S(1)}, f32[2,256,256]{2,1,0:T(8,128)}, u32[]{:S(2)}) copy-start(f32[2,256,256]{2,1,0:T(8,128)} %own.3) | copy-start | bytes 1572868
  1.7 12.0 %copy-start.3 = (f32[2,256,256]{2,1,0:T(8,128)S(1)}, f32[2,256,256]{2,1,0:T(8,128)}, u32[]{:S(2)}) copy-start(f32[2,256,256]{2,1,0:T(8,128)} %refs_8_.3) | copy-start | bytes 1572868
  13.7 0.7 copy-start.6
  14.3 1.1 %copy-start.1 = (bf16[1,1,6,256,256]{4,3,2,1,0:T(8,128)(2,1)S(1)}, bf16[1,1,6,256,256]{4,3,2,1,0:T(8,128)(2,1)}, u32[]{:S(2)}) copy-start(bf16[1,1,6,256,256]{4,3,2,1,0:T(8,128)(2,1)} %param.8) | copy-start | bytes 2359300
  15.5 0.9 %copy-start.4 = (bf16[2,256,256]{2,1,0:T(8,128)(2,1)S(1)}, bf16[2,256,256]{2,1,0:T(8,128)(2,1)}, u32[]{:S(2)}) copy-start(bf16[2,256,256]{2,1,0:T(8,128)(2,1)} %constant.2.clone.refs_10_) | copy-start | bytes 786436
  24.9 31.7 %copy-start.2 = (bf16[1,1,6,256,256]{4,3,2,1,0:T(8,128)(2,1)S(1)}, bf16[1,1,6,256,256]{4,3,2,1,0:T(8,128)(2,1)}, u32[]{:S(2)}) copy-start(bf16[1,1,6,256,256]{4,3,2,1,0:T(8,128)(2,1)} %param.8) | copy-start | bytes 2359300
  44.9 11.7 %copy-start.5 = (bf16[2,256,256]{2,1,0:T(8,128)(2,1)S(1)}, bf16[2,256,256]{2,1,0:T(8,128)(2,1)}, u32[]{:S(2)}) copy-start(bf16[2,256,256]{2,1,0:T(8,128)(2,1)} %constant.2.clone.refs_10_) | copy-start | bytes 786436
where the time goes:
time: 81.6 us; the launch traced here: 80.5 us
  Pallas kernels  75.1 us (92%)
  local copies, waits for them, and re-layouts  4.59 us (6%)
    pallas_call x2, Pallas kernels, per_device(): pl.pallas_call(functools.partial(update_kernel, first), out_shape=shapes,...  34.8 us
    pallas_call x2, Pallas kernels, per_device(): pl.pallas_call(halo_kernel, out_shape=edge_shapes, in_specs=vmem(1), out_...  23.6 us
    pallas_call x2, Pallas kernels, per_device(): pl.pallas_call(functools.partial(gradient_kernel, planes), out_shape=[f32...  16.7 us
    unnamed x15, local copies, waits for them, and re-layouts  4.59 us

commit v1 on v0

v1 whole, which is shorter than its diff:
```python
import functools
import math

import jax
import jax.numpy as jnp
import numpy as np
from jax import lax
from jax.experimental import pallas as pl
from jax.experimental.pallas import tpu as pltpu
from jax.sharding import PartitionSpec as P

TILE = 256
RIM = 128
MAXPOS = 6
ITERS = 2
LANES = 128
HALF = 128
CHUNK = 32
VMEM_LIMIT = 28 * 1024 * 1024
WIRE_COST = pl.CostEstimate(flops=0, transcendentals=0, bytes_accessed=40_000_000)

smooth_term = 0.25
step_size = 0.5
regular_term = 1.0

AXES = ("row", "col")
SIDES = [(-1, 0), (1, 0), (0, -1), (0, 1), (-1, -1), (-1, 1), (1, -1), (1, 1)]
CORNERS = SIDES[4:]


def dft_tables():
    positions = np.arange(TILE)
    phase_step = (positions[:, None] * positions[None, :]) % TILE
    angle = phase_step.astype(np.float32) * np.float32(2.0 * math.pi / TILE)
    scale = np.float32(1.0 / math.sqrt(TILE))
    real = np.cos(angle).astype(np.float32) * scale
    imag = -np.sin(angle).astype(np.float32) * scale
    left, right = [], []
    for parity in range(2):
        r = real[parity::2, :HALF]
        i = imag[parity::2, :HALF]
        m = np.block([[r, -i], [i, r]])
        left.append(m)
        right.append(m.T)
    return np.stack(left + right).astype(jnp.bfloat16)


def order_table():
    picked = np.concatenate([np.arange(0, TILE, 2), np.arange(1, TILE, 2)])
    table = np.zeros((TILE, TILE), np.float32)
    table[np.arange(TILE), picked] = 1.0
    return np.stack([table, table.T]).astype(jnp.bfloat16)


def edge(step, length):
    if step < 0:
        return slice(0, RIM)
    if step > 0:
        return slice(length - RIM, length)
    return slice(0, length)


def zone(step):
    return (slice(0, RIM), slice(RIM, RIM + TILE), slice(RIM + TILE, 2 * RIM + TILE))[step + 1]


def rim_block(right):
    return 0 if right < 0 else 3


def own_block(right):
    return 1 if right < 0 else 2


def inside(row, col):
    rows, cols = lax.axis_size("row"), lax.axis_size("col")
    return (row >= 0) & (row < rows) & (col >= 0) & (col < cols)


def greet(row, col):
    barrier = pltpu.get_barrier_semaphore()
    peers = 0
    for down, right in SIDES[:4]:
        present = inside(row + down, col + right)
        peers = peers + jnp.where(present, 1, 0)

        @pl.when(present)
        def _():
            pl.semaphore_signal(
                barrier,
                inc=1,
                device_id=(row + down, col + right),
                device_id_type=pl.DeviceIdType.MESH,
            )

    pl.semaphore_wait(barrier, peers)


def transfer(source, landing, sends, receives, slot, device):
    return pltpu.make_async_remote_copy(
        src_ref=source,
        dst_ref=landing,
        send_sem=sends.at[slot],
        recv_sem=receives.at[slot],
        device_id=device,
        device_id_type=pl.DeviceIdType.MESH,
    )


def half_slot(down, right):
    return (0 if down < 0 else 1) + (0 if right < 0 else 8)


def halo_copies(source, ext, sends, receives):
    def row_copy(down, right, device):
        return transfer(
            source(down, right),
            ext.at[:, own_block(right), zone(-down), :],
            sends,
            receives,
            half_slot(down, right),
            device,
        )

    def col_copy(right, device):
        at = SIDES.index((0, right))
        return transfer(
            source(0, right),
            ext.at[:, rim_block(-right), zone(0), :],
            sends,
            receives,
            at,
            device,
        )

    def corner_copy(down, right, device):
        at = SIDES.index((down, right))
        return transfer(
            ext.at[:, own_block(right), zone(-down), :],
            ext.at[:, rim_block(-right), zone(-down), :],
            sends,
            receives,
            at,
            device,
        )

    return row_copy, col_copy, corner_copy


def halo_begin(copies, row, col):
    row_copy, col_copy, _ = copies
    for down, right in CORNERS:

        @pl.when(inside(row + down, col))
        def _():
            row_copy(down, right, (row + down, col)).start()

    for right in (-1, 1):

        @pl.when(inside(row, col + right))
        def _():
            col_copy(right, (row, col + right)).start()


def blank_outside(ext, row, col):
    for down, right in SIDES:

        @pl.when(jnp.logical_not(inside(row - down, col - right)))
        def _():
            blocks = slice(1, 3) if right == 0 else slice(rim_block(-right), rim_block(-right) + 1)
            part = ext.at[:, blocks, zone(-down), :]
            part[...] = jnp.zeros(part.shape, jnp.float32)


def halo_finish(copies, row, col):
    row_copy, col_copy, corner_copy = copies
    for down, right in CORNERS:

        @pl.when(inside(row - down, col))
        def _():
            row_copy(down, right, (row - down, col)).wait_recv()

        @pl.when(inside(row - down, col) & inside(row, col + right))
        def _():
            corner_copy(down, right, (row, col + right)).start()

    for right in (-1, 1):

        @pl.when(inside(row, col - right))
        def _():
            col_copy(right, (row, col - right)).wait_recv()

    for down, right in CORNERS:

        @pl.when(inside(row - down, col - right))
        def _():
            corner_copy(down, right, (row, col - right)).wait_recv()

    for down, right in CORNERS:

        @pl.when(inside(row + down, col))
        def _():
            row_copy(down, right, (row + down, col)).wait_send()

        @pl.when(inside(row - down, col) & inside(row, col + right))
        def _():
            corner_copy(down, right, (row, col + right)).wait_send()

    for right in (-1, 1):

        @pl.when(inside(row, col + right))
        def _():
            col_copy(right, (row, col + right)).wait_send()


def prepare(offs, probe, amps, order, turned, sorted_amps, swap):
    lane = lax.broadcasted_iota(jnp.int32, (CHUNK, LANES), 1)

    def one_slot(slot, carry):
        left = offs[1, slot] % TILE
        shift = left % LANES
        low = jnp.where(lane >= shift, 1, 0)
        straight = low != left // LANES
        for p in range(2):
            for at in range(0, TILE, CHUNK):
                rows = slice(at, at + CHUNK)
                a = pltpu.roll(probe[p, rows, :LANES], shift, 1)
                b = pltpu.roll(probe[p, rows, LANES:], shift, 1)
                turned[slot, p, 0, rows, :] = jnp.where(straight, a, b)
                turned[slot, p, 1, rows, :] = jnp.where(straight, b, a)
        swap[...] = jnp.dot(order[0], amps[slot], preferred_element_type=jnp.float32).astype(jnp.bfloat16)
        placed = jnp.dot(swap[...], order[1], preferred_element_type=jnp.float32).astype(jnp.bfloat16)
        sorted_amps[slot, 0] = placed[:, :LANES]
        sorted_amps[slot, 1] = placed[:, LANES:]
        return carry

    lax.fori_loop(0, MAXPOS, one_slot, 0)


def halo_kernel(offs, field, probe, amps, order, ext, turned, sorted_amps, swap, sends, receives):
    row, col = lax.axis_index("row"), lax.axis_index("col")
    greet(row, col)

    def source(down, right):
        cols = slice(0, LANES) if right < 0 else slice(LANES, 2 * LANES)
        return field.at[:, edge(down, TILE), cols]

    copies = halo_copies(source, ext, sends, receives)
    halo_begin(copies, row, col)
    blank_outside(ext, row, col)
    for block in range(2):
        ext[:, 1 + block, RIM : RIM + TILE, :] = field[:, :, block * LANES : (block + 1) * LANES]
    prepare(offs, probe, amps, order, turned, sorted_amps, swap)
    halo_finish(copies, row, col)


def gradient_kernel(planes, offs, cnt, ext, turned, amps, mats, canvas, *scratch):
    canvas[...] = jnp.zeros_like(canvas)
    lane = lax.broadcasted_iota(jnp.int32, (CHUNK, LANES), 1)
    bf16 = jnp.bfloat16

    def product(a, b):
        return jnp.dot(a, b, preferred_element_type=jnp.float32)

    def stages(slot, used, buffers):
        waves, halves, spectra = buffers
        top = offs[0, slot]
        left = offs[1, slot]
        near = [lane >= left - b * LANES for b in range(2)]

        def gather():
            for at in range(0, HALF, CHUNK):
                for b in range(2):
                    cols = slice(b * LANES, (b + 1) * LANES)
                    parts = []
                    for far in (0, HALF):
                        rows = pl.ds(top + at + far, CHUNK)
                        wr, wi = [
                            jnp.where(near[b], ext[p, b, rows, :], ext[p, b + 2, rows, :])
                            for p in range(2)
                        ]
                        pr = turned[slot, 0, b, at + far : at + far + CHUNK, :]
                        pi = turned[slot, 1, b, at + far : at + far + CHUNK, :]
                        parts.append((pr * wr - pi * wi, pr * wi + pi * wr))
                    for p in range(2):
                        rows = slice(p * HALF + at, p * HALF + at + CHUNK)
                        waves[0, rows, cols] = (parts[0][p] + parts[1][p]).astype(bf16)
                        waves[1, rows, cols] = (parts[0][p] - parts[1][p]).astype(bf16)

        def forward_rows():
            for parity in range(2):
                y = product(mats[parity], waves[parity])
                a, b = y[:, :LANES], y[:, LANES:]
                rows = slice(parity * HALF, (parity + 1) * HALF)
                for at, z in enumerate((a + b, a - b)):
                    halves[at, rows, :LANES] = z[:HALF].astype(bf16)
                    halves[at, rows, LANES:] = z[HALF:].astype(bf16)

        def forward_cols():
            for parity in range(2):
                spectra[parity] = product(halves[parity], mats[2 + parity])

        def residual():
            for parity in range(2):
                for at in range(0, TILE, CHUNK):
                    sr = spectra[parity, at : at + CHUNK, :LANES]
                    si = spectra[parity, at : at + CHUNK, LANES:]
                    amp = amps[slot, parity, at : at + CHUNK, :].astype(jnp.float32)
                    factor = 1.0 - amp * lax.rsqrt(sr * sr + si * si + smooth_term)
                    if used is not None:
                        factor = jnp.where(used, factor, 0.0)
                    odd, inner = divmod(at, HALF)
                    cols = slice(parity * LANES, (parity + 1) * LANES)
                    waves[odd, inner : inner + CHUNK, cols] = (sr * factor).astype(bf16)
                    waves[odd, HALF + inner : HALF + inner + CHUNK, cols] = (si * factor).astype(bf16)

        def back_rows():
            e = product(mats[2], waves[0])
            o = product(mats[3], waves[1])
            for at, z in enumerate((e + o, e - o)):
                rows = slice(at * HALF, (at + 1) * HALF)
                for parity in range(2):
                    cols = slice(parity * LANES, (parity + 1) * LANES)
                    halves[parity, rows, :LANES] = z[:HALF, cols].astype(bf16)
                    halves[parity, rows, LANES:] = z[HALF:, cols].astype(bf16)

        def back_cols():
            for parity in range(2):
                spectra[parity] = product(halves[parity], mats[parity])

        def scatter():
            for at in range(0, TILE, CHUNK):
                rows = pl.ds(top + at, CHUNK)
                er, ei = [spectra[0, at : at + CHUNK, p * LANES : (p + 1) * LANES] for p in range(2)]
                pr_, pi_ = [spectra[1, at : at + CHUNK, p * LANES : (p + 1) * LANES] for p in range(2)]
                for b in range(2):
                    br, bi = (er + pr_, ei + pi_) if b == 0 else (er - pr_, ei - pi_)
                    pr = turned[slot, 0, b, at : at + CHUNK, :]
                    pi = turned[slot, 1, b, at : at + CHUNK, :]
                    pieces = [pr * br + pi * bi, pr * bi - pi * br]
                    if planes > 2:
                        light = pr * pr + pi * pi
                        pieces.append(light if used is None else jnp.where(used, light, 0.0))
                    for p, piece in enumerate(pieces):
                        canvas[p, b, rows, :] += jnp.where(near[b], piece, 0.0)
                        canvas[p, b + 2, rows, :] += jnp.where(near[b], 0.0, piece)

        return [gather, forward_rows, forward_cols, residual, back_rows, back_cols, scatter]

    first, second = scratch[:3], scratch[3:]

    def two_slots(pair, carry):
        a = stages(2 * pair, None, first)
        b = stages(2 * pair + 1, 2 * pair + 1 < cnt[0], second)
        a[0]()
        for at in range(1, len(a)):
            a[at]()
            b[at - 1]()
        b[-1]()
        return carry

    lax.fori_loop(0, (cnt[0] + 1) // 2, two_slots, 0)


def update_kernel(first, canvas, ext, *refs):
    if first:
        new, scale_out = refs[:2]
        halo_sems = refs[-2:]
        refs = refs[2:-2]
    else:
        scale_in, new = refs[:2]
        refs = refs[2:]
    land_corner, land_col, land_row, total, sends, receives = refs
    row, col = lax.axis_index("row"), lax.axis_index("col")
    greet(row, col)

    def corner_copy(down, right, device):
        at = SIDES.index((down, right))
        return transfer(
            canvas.at[:, rim_block(right), zone(down), :],
            land_corner.at[at - 4],
            sends,
            receives,
            at,
            device,
        )

    def col_copy(right, device):
        at = SIDES.index((0, right))
        return transfer(
            canvas.at[:, rim_block(right), zone(0), :], land_col.at[at - 2], sends, receives, at, device
        )

    def row_copy(down, right, device):
        vertical = 0 if down < 0 else 1
        return transfer(
            total.at[:, own_block(right) - 1, zone(down), :],
            land_row.at[vertical, :, own_block(right) - 1],
            sends,
            receives,
            half_slot(down, right),
            device,
        )

    for down, right in CORNERS:

        @pl.when(inside(row + down, col + right))
        def _():
            corner_copy(down, right, (row, col + right)).start()

    for right in (-1, 1):

        @pl.when(inside(row, col + right))
        def _():
            col_copy(right, (row, col + right)).start()

    total[...] = canvas[:, 1:3]

    def send_half(side):
        block = own_block(side) - 1
        for down in (-1, 1):

            @pl.when(inside(row + down, col) & inside(row, col + side))
            def _():
                corner_copy(down, -side, (row, col + side)).wait_recv()
                total[:, block, zone(down), :] += land_corner[SIDES.index((down, -side)) - 4]

            @pl.when(inside(row + down, col))
            def _():
                row_copy(down, side, (row + down, col)).start()

    @pl.when(col % 2 == 1)
    def _():
        send_half(-1)
        send_half(1)

    @pl.when(col % 2 == 0)
    def _():
        send_half(1)
        send_half(-1)

    for right in (-1, 1):

        @pl.when(inside(row, col - right))
        def _():
            col_copy(right, (row, col - right)).wait_recv()
            total[:, own_block(-right) - 1, zone(0), :] += land_col[SIDES.index((0, right)) - 2]

    for down, right in CORNERS:

        @pl.when(inside(row - down, col))
        def _():
            row_copy(down, right, (row - down, col)).wait_recv()
            part = slice(RIM, 2 * RIM) if down > 0 else slice(TILE, TILE + RIM)
            total[:, own_block(right) - 1, part, :] += land_row[0 if down < 0 else 1, :, own_block(right) - 1]

    for down, right in CORNERS:

        @pl.when(inside(row + down, col + right))
        def _():
            corner_copy(down, right, (row, col + right)).wait_send()

        @pl.when(inside(row + down, col))
        def _():
            row_copy(down, right, (row + down, col)).wait_send()

    for right in (-1, 1):

        @pl.when(inside(row, col + right))
        def _():
            col_copy(right, (row, col + right)).wait_send()

    for block in range(2):
        if first:
            scale = step_size / (total[2, block, zone(0), :] + regular_term)
            scale_out[block] = scale
        else:
            scale = scale_in[block]
        for p in range(2):
            value = ext[p, 1 + block, zone(0), :] - total[p, block, zone(0), :] * scale
            if first:
                new[p, 1 + block, zone(0), :] = value
            else:
                new[p, :, block * LANES : (block + 1) * LANES] = value

    if first:

        def source(down, right):
            part = {-1: slice(RIM, 2 * RIM), 0: zone(0), 1: slice(TILE, TILE + RIM)}[down]
            return new.at[:, own_block(right), part, :]

        copies = halo_copies(source, new, *halo_sems)
        halo_begin(copies, row, col)
        blank_outside(new, row, col)
        halo_finish(copies, row, col)


def vmem(count):
    return [pl.BlockSpec(memory_space=pltpu.VMEM)] * count


def smem(count):
    return [pl.BlockSpec(memory_space=pltpu.SMEM)] * count


def dma_sems():
    return [pltpu.SemaphoreType.DMA((10,))] * 2


def f32(*shape):
    return jax.ShapeDtypeStruct(shape, jnp.float32)


def wire_params(identity):
    return pltpu.CompilerParams(
        collective_id=identity, has_side_effects=True, vmem_limit_bytes=VMEM_LIMIT
    )


def gradient(planes, offs, cnt, ext, turned, amps, mats):
    slot_scratch = [
        pltpu.VMEM((2, TILE, TILE), jnp.bfloat16),
        pltpu.VMEM((2, TILE, TILE), jnp.bfloat16),
        pltpu.VMEM((2, TILE, TILE), jnp.float32),
    ]
    return pl.pallas_call(
        functools.partial(gradient_kernel, planes),
        out_shape=f32(planes, 4, 2 * TILE, LANES),
        in_specs=smem(2) + vmem(4),
        out_specs=vmem(1)[0],
        scratch_shapes=slot_scratch * 2,
        compiler_params=pltpu.CompilerParams(vmem_limit_bytes=VMEM_LIMIT),
        name=f"gradient{planes}",
    )(offs, cnt, ext, turned, amps, mats)


def halo(offs, field, probe, amps, order):
    return pl.pallas_call(
        halo_kernel,
        out_shape=[
            f32(2, 4, 2 * TILE, LANES),
            f32(MAXPOS, 2, 2, TILE, LANES),
            jax.ShapeDtypeStruct((MAXPOS, 2, TILE, LANES), jnp.bfloat16),
        ],
        in_specs=smem(1) + vmem(4),
        out_specs=vmem(3),
        scratch_shapes=[pltpu.VMEM((TILE, TILE), jnp.bfloat16)] + dma_sems(),
        compiler_params=wire_params(0),
        cost_estimate=WIRE_COST,
        name="halo",
    )(offs, field, probe, amps, order)


def update(planes, canvas, ext, scale):
    first = scale is None
    if first:
        shapes = [f32(2, 4, 2 * TILE, LANES), f32(2, TILE, LANES)]
    else:
        shapes = [f32(2, TILE, TILE)]
    operands = [canvas, ext] + ([] if first else [scale])
    return pl.pallas_call(
        functools.partial(update_kernel, first),
        out_shape=shapes,
        in_specs=vmem(len(operands)),
        out_specs=vmem(len(shapes)),
        scratch_shapes=[
            pltpu.VMEM((4, planes, HALF, LANES), jnp.float32),
            pltpu.VMEM((2, planes, TILE, LANES), jnp.float32),
            pltpu.VMEM((2, planes, 2, HALF, LANES), jnp.float32),
            pltpu.VMEM((planes, 2, 2 * TILE, LANES), jnp.float32),
        ]
        + dma_sems() * (2 if first else 1),
        compiler_params=wire_params(1 if first else 2),
        cost_estimate=WIRE_COST,
        name="exchange" if first else "finish",
    )(*operands)


def per_device(object_field, probe_field, amplitudes, offsets, counts):
    mats = jnp.asarray(dft_tables())
    order = jnp.asarray(order_table())
    offs = offsets.reshape(MAXPOS, 2).T
    cnt = counts.reshape(1)
    amps = amplitudes.reshape(MAXPOS, TILE, TILE)
    ext, turned, amps = halo(offs, object_field, probe_field, amps, order)
    scale = None
    for iteration in range(ITERS):
        planes = 3 if iteration == 0 else 2
        canvas = gradient(planes, offs, cnt, ext, turned, amps, mats)
        if iteration == 0:
            ext, scale = update(planes, canvas, ext, None)
        else:
            (field,) = update(planes, canvas, ext, scale)
    return field


def solution(mesh):
    in_specs = (
        P(None, "row", "col"),
        P(),
        P("row", "col", None, None, None),
        P("row", "col", None, None),
        P("row", "col"),
    )
    out_specs = P(None, "row", "col")
    return jax.shard_map(
        per_device, mesh=mesh, in_specs=in_specs, out_specs=out_specs, check_vma=False
    )
```

time: 81.6 us -> 70.2 us (0.86)
  Pallas kernels: 75.1 us -> 62.8 us
  local copies, waits for them, and re-layouts: 4.59 us -> 5.64 us
    pallas_call x6 -> x5, Pallas kernels: 75.1 us -> 62.8 us  [the longest x2 41.8 us: update(): pl.pallas_call(functools.partial(update_kernel, first), out_shape=shapes,...]
    unnamed x15 -> x13, local copies, waits for them, and re-layouts: 4.59 us -> 5.64 us
where the time goes in v1:
time: 70.2 us; the launch traced here: 69.2 us
  Pallas kernels  62.8 us (89%)
  local copies, waits for them, and re-layouts  5.64 us (8%)
  between operations  0.77 us (1%)
    pallas_call x2, Pallas kernels, update(): pl.pallas_call(functools.partial(update_kernel, first), out_shape=shapes,...  41.8 us
    pallas_call x1, Pallas kernels, halo(): pl.pallas_call(halo_kernel, out_shape=[f32(2, 4, 2 * TILE, LANES), f32(MA...  12.6 us
    pallas_call x2, Pallas kernels, gradient(): pl.pallas_call(functools.partial(gradient_kernel, planes), out_shape=f32(...  8.48 us
    unnamed x13, local copies, waits for them, and re-layouts  5.64 us

profile of v1, /device:TPU:9, one launch (start us, length us, event | category | flops | bytes accessed | tf_op | source)
XLA Modules:
  0.0 69.2 jit_solution(5947321855454478517)
XLA Ops:
  0.0 0.0 copy-start
  0.7 0.0 copy-start.1
  0.7 1.1 %copy-done.1 = bf16[1,1,6,256,256]{4,3,2,1,0:T(8,128)(2,1)S(1)} copy-done((bf16[1,1,6,256,256]{4,3,2,1,0:T(8,128)(2,1)S(1)}, bf16[1,1,6,256,256]{4,3,2,1,0:T(8,128)(2,1)}, u32[]{:S(2)}) %copy-start.1) | copy-done | bytes 786456
  1.8 0.0 copy-start.2
  1.9 1.0 %copy-done.2 = f32[2,256,256]{2,1,0:T(8,128)S(1)} copy-done((f32[2,256,256]{2,1,0:T(8,128)S(1)}, f32[2,256,256]{2,1,0:T(8,128)}, u32[]{:S(2)}) %copy-start.2) | copy-done | bytes 524312
  2.9 0.0 copy-start.3
  2.9 1.0 %copy-done.3 = f32[2,256,256]{2,1,0:T(8,128)S(1)} copy-done((f32[2,256,256]{2,1,0:T(8,128)S(1)}, f32[2,256,256]{2,1,0:T(8,128)}, u32[]{:S(2)}) %copy-start.3) | copy-done | bytes 524312
  3.9 0.0 copy-start.4
  3.9 0.9 %copy-done.4 = bf16[2,256,256]{2,1,0:T(8,128)(2,1)S(1)} copy-done((bf16[2,256,256]{2,1,0:T(8,128)(2,1)S(1)}, bf16[2,256,256]{2,1,0:T(8,128)(2,1)}, u32[]{:S(2)}) %copy-start.4) | copy-done | bytes 262168
  4.9 0.0 copy-start.5
  4.9 0.7 copy-done.5
  5.6 12.6 %halo.1 = (f32[2,4,512,128]{3,2,1,0:T(8,128)S(1)}, f32[6,2,2,256,128]{4,3,2,1,0:T(8,128)S(1)}, bf16[6,2,256,128]{3,2,1,0:T(8,128)(2,1)S(1)}) custom-call(s32[2,6]{1,0:T(2,128)S(1)} %bitcast.8, f32[2,256,256]{2,1,0:T(8,128)S(1)} %copy-done.2, f32[2,256,256]{2,1,0:T(8,128)S(1)} %copy-done.3, bf16[6,256,256]{2,1,0:T(8,128)(2,1)S(1)} %bitcast.7, ...), custom_call_target="tpu_custom_call" | custom-call | bytes 40000000 | tf_op jit(solution)/shard_map/halo/pallas_call | solution.py:538
  18.1 0.0 copy-done
  18.1 4.4 %gradient3.1.canvas = f32[3,4,512,128]{3,2,1,0:T(8,128)S(1)} custom-call(s32[2,6]{1,0:T(2,128)S(1)} %bitcast.9, s32[1]{0:T(128)} %bitcast.5.cnt, f32[2,4,512,128]{3,2,1,0:T(8,128)S(1)} %get-tuple-element.10.ext, f32[6,2,2,256,128]{4,3,2,1,0:T(8,128)S(1)} %get-tuple-element.11.turned, bf16[6,2,256,128]{3,2,1,0:T(8,128)(2,1)S(1)} %get-tuple-element.12.amps, ...), custom_call_target="tpu_custom_call" | custom-call | tf_op jit(solution)/shard_map/gradient3/pallas_call | solution.py:526
  22.5 28.8 %exchange.1 = (f32[2,4,512,128]{3,2,1,0:T(8,128)S(1)}, f32[2,256,128]{2,1,0:T(8,128)S(1)}) custom-call(f32[3,4,512,128]{3,2,1,0:T(8,128)S(1)} %gradient3.1.canvas, f32[2,4,512,128]{3,2,1,0:T(8,128)S(1)} %get-tuple-element.10.ext), custom_call_target="tpu_custom_call" | custom-call | bytes 40000000 | tf_op jit(solution)/shard_map/exchange/pallas_call | solution.py:561
  51.4 4.1 %gradient2.1.canvas = f32[2,4,512,128]{3,2,1,0:T(8,128)S(1)} custom-call(s32[2,6]{1,0:T(2,128)S(1)} %bitcast.10, s32[1]{0:T(128)} %bitcast.6.cnt, f32[2,4,512,128]{3,2,1,0:T(8,128)S(1)} %get-tuple-element.13.ext, f32[6,2,2,256,128]{4,3,2,1,0:T(8,128)S(1)} %get-tuple-element.11.turned, bf16[6,2,256,128]{3,2,1,0:T(8,128)(2,1)S(1)} %get-tuple-element.12.amps, ...), custom_call_target="tpu_custom_call" | custom-call | tf_op jit(solution)/shard_map/gradient2/pallas_call | solution.py:526
  55.5 12.9 %finish.1 = f32[2,256,256]{2,1,0:T(8,128)S(1)} custom-call(f32[2,4,512,128]{3,2,1,0:T(8,128)S(1)} %gradient2.1.canvas, f32[2,4,512,128]{3,2,1,0:T(8,128)S(1)} %get-tuple-element.13.ext, f32[2,256,128]{2,1,0:T(8,128)S(1)} %get-tuple-element.14.refs_0_), custom_call_target="tpu_custom_call" | custom-call | bytes 40000000 | tf_op jit(solution)/shard_map/finish/pallas_call | solution.py:561
  68.4 0.8 %copy.10 = f32[2,256,256]{2,1,0:T(8,128)} copy(f32[2,256,256]{2,1,0:T(8,128)S(1)} %finish.1) | data formatting | bytes 1048576
Async XLA Ops:
  0.0 18.1 %copy-start = (bf16[4,256,256]{2,1,0:T(8,128)(2,1)S(1)}, bf16[4,256,256]{2,1,0:T(8,128)(2,1)}, u32[]{:S(2)}) copy-start(bf16[4,256,256]{2,1,0:T(8,128)(2,1)} %constant.4.clone.mats) | copy-start | bytes 1572868
  0.7 1.1 %copy-start.1 = (bf16[1,1,6,256,256]{4,3,2,1,0:T(8,128)(2,1)S(1)}, bf16[1,1,6,256,256]{4,3,2,1,0:T(8,128)(2,1)}, u32[]{:S(2)}) copy-start(bf16[1,1,6,256,256]{4,3,2,1,0:T(8,128)(2,1)} %param.9) | copy-start | bytes 2359300
  1.8 1.0 %copy-start.2 = (f32[2,256,256]{2,1,0:T(8,128)S(1)}, f32[2,256,256]{2,1,0:T(8,128)}, u32[]{:S(2)}) copy-start(f32[2,256,256]{2,1,0:T(8,128)} %field.1) | copy-start | bytes 1572868
  2.9 1.0 %copy-start.3 = (f32[2,256,256]{2,1,0:T(8,128)S(1)}, f32[2,256,256]{2,1,0:T(8,128)}, u32[]{:S(2)}) copy-start(f32[2,256,256]{2,1,0:T(8,128)} %probe.1) | copy-start | bytes 1572868
  3.9 0.9 %copy-start.4 = (bf16[2,256,256]{2,1,0:T(8,128)(2,1)S(1)}, bf16[2,256,256]{2,1,0:T(8,128)(2,1)}, u32[]{:S(2)}) copy-start(bf16[2,256,256]{2,1,0:T(8,128)(2,1)} %constant.5.clone.order) | copy-start | bytes 786436
  4.9 0.7 copy-start.5
